TPU v7x, 32 devices: a whole 2x2x4 slice. The times are simulated.
32 devices in a mesh: roll: 8 (over z, core), kvh: 4 (over y, x).
Axes of the slice: x: 2, y: 2, z: 4, core: 2. Of those that a mesh axis runs over, the one named last changes fastest.
Arguments:
- out_grad: bfloat16 [8, 256, 5120], P('roll', 'kvh'), may hold values from -48 to 48
- out_weight: bfloat16 [4, 5, 128, 5120], P('kvh'), may hold values from -0.078125 to 0.078125
- queries: bfloat16 [8, 256, 4, 5, 128], P('roll', None, 'kvh'), may hold values from -16 to 16
- keys_new: bfloat16 [8, 256, 4, 128], P('roll', None, 'kvh'), may hold values from -16 to 16
- values_new: bfloat16 [8, 256, 4, 128], P('roll', None, 'kvh'), may hold values from -6 to 6
- keys_prompt: bfloat16 [2048, 4, 128], P('roll', 'kvh'), may hold values from -6 to 6
- values_prompt: bfloat16 [2048, 4, 128], P('roll', 'kvh'), may hold values from -6 to 6
- offsets: int32 [8], P('roll'), may hold values from 0 to 3840
Outputs:
- grad_queries: bfloat16 [8, 256, 4, 5, 128], P('roll', None, 'kvh')
- grad_keys_new: bfloat16 [8, 256, 4, 128], P('roll', None, 'kvh')
- grad_values_new: bfloat16 [8, 256, 4, 128], P('roll', None, 'kvh')
- grad_keys_prompt: bfloat16 [2048, 4, 128], P('roll', 'kvh')
- grad_values_prompt: bfloat16 [2048, 4, 128], P('roll', 'kvh')
Inputs may be any that keep to these rules, and one draw needn't show every extreme that they name: `offsets`: each slice lies inside a response of 4096 tokens.
All inputs are finite; a program needn't handle non-finite values.
Results may differ from a plain program's by a relative error of at most 0.015.
The roundings to bfloat16 on the way count: a program that leaves them out, or rounds other values in their place, can miss the bound.
Values may be sent and summed in bfloat16 or wider, within the bound.
No kernel may reach another device: no remote copies, remote signals or barrier semaphores. Data moves between devices by JAX's collectives and lax.ppermute only.
A program may use at most 64 MiB of HBM per device.

v0:
```python
import math

import jax
import jax.numpy as jnp
from jax import lax
from jax.sharding import PartitionSpec as P

theta_base = 1000000.0


def rotation(positions, head_width):
    half_width = head_width // 2
    frequency = jnp.power(theta_base, -(jnp.arange(half_width, dtype=jnp.float32) / half_width))
    angles = positions.astype(jnp.float32)[:, None] * frequency[None, :]
    return (jnp.cos(angles), jnp.sin(angles))


def rotate(vectors, cos_part, sin_part, direction):
    half_width = vectors.shape[-1] // 2
    front_half = vectors[..., :half_width]
    back_half = vectors[..., half_width:]
    return jnp.concatenate(
        [
            front_half * cos_part - direction * back_half * sin_part,
            back_half * cos_part + direction * front_half * sin_part,
        ],
        axis=-1,
    )


def inner_dot(left, right):
    return lax.dot_general(
        left, right, (((1,), (1,)), ((), ())), preferred_element_type=jnp.float32
    )


def outer_sum(left, right):
    return lax.dot_general(
        left, right, (((0,), (0,)), ((), ())), preferred_element_type=jnp.float32
    )


def block_grads(context, key_block, value_block):
    query_rows, grad_rows, log_total, row_delta, score_scale = context
    scores = inner_dot(query_rows, key_block) * score_scale
    attn_probs = jnp.exp(scores - log_total[:, None]).astype(jnp.bfloat16)
    prob_grad = inner_dot(grad_rows, value_block)
    score_grad = (
        attn_probs.astype(jnp.float32) * (prob_grad - row_delta[:, None]) * score_scale
    ).astype(jnp.bfloat16)
    return (attn_probs, score_grad)


def prompt_terms(context, key_rows, value_rows):
    row_count, head_width = key_rows.shape
    block_len = math.gcd(row_count, 512)
    key_blocks = key_rows.reshape(row_count // block_len, block_len, head_width)
    value_blocks = value_rows.reshape(row_count // block_len, block_len, head_width)

    def term_step(unused, blocks):
        attn_probs, score_grad = block_grads(context, blocks[0], blocks[1])
        return (
            unused,
            jnp.stack(
                [outer_sum(score_grad, context[0]), outer_sum(attn_probs, context[1])], axis=1
            ),
        )

    unused, block_terms = lax.scan(
        term_step, jnp.zeros((), jnp.float32), (key_blocks, value_blocks)
    )
    return block_terms.reshape(row_count, 2, head_width)


def local(out_grad, out_weight, queries, keys_new, values_new, keys_prompt, values_prompt, offsets):
    roll_local, seq_len, kv_local, group_size, head_width = queries.shape
    prompt_local = keys_prompt.shape[0]
    prompt_total = prompt_local * lax.axis_size("roll")
    score_scale = head_width ** (-0.5)
    row_total = roll_local * seq_len * group_size
    attn_grad = jnp.einsum(
        "rsc,ghdc->rsghd",
        lax.all_gather(out_grad, "kvh", axis=1, tiled=True),
        out_weight,
        preferred_element_type=jnp.float32,
    ).astype(jnp.bfloat16)
    cached_keys, cached_values = (
        lax.all_gather(keys_prompt, "roll", axis=0, tiled=True),
        lax.all_gather(values_prompt, "roll", axis=0, tiled=True),
    )
    positions = prompt_total + offsets[:, None] + jnp.arange(seq_len, dtype=jnp.int32)[None, :]
    cos_flat, sin_flat = rotation(positions.reshape(-1), head_width)
    cos_four = cos_flat.reshape(roll_local, seq_len, 1, head_width // 2)
    sin_four = sin_flat.reshape(roll_local, seq_len, 1, head_width // 2)
    query_rot = rotate(
        queries.astype(jnp.float32), cos_four[:, :, :, None], sin_four[:, :, :, None], 1.0
    ).astype(jnp.bfloat16)
    key_rot = rotate(keys_new.astype(jnp.float32), cos_four, sin_four, 1.0).astype(jnp.bfloat16)
    block_len = math.gcd(prompt_total, 512)
    block_count = prompt_total // block_len
    causal = (jnp.arange(seq_len)[None, :] <= jnp.arange(seq_len)[:, None])[None, :, None, :]
    head_index = 0
    query_head = query_rot[:, :, head_index]
    key_head = key_rot[:, :, head_index]
    value_head = values_new[:, :, head_index]
    grad_head = attn_grad[:, :, head_index]
    query_rows = query_head.reshape(row_total, head_width)
    grad_rows = grad_head.reshape(row_total, head_width)
    key_blocks = cached_keys[:, head_index].reshape(block_count, block_len, head_width)
    value_blocks = cached_values[:, head_index].reshape(block_count, block_len, head_width)
    near_scores = (
        jnp.einsum("rshd,rtd->rsht", query_head, key_head, preferred_element_type=jnp.float32)
        * score_scale
    )
    near_scores = jnp.where(causal, near_scores, -jnp.inf)
    near_max = jnp.max(near_scores, axis=3, keepdims=True)
    near_sum = jnp.sum(jnp.exp(near_scores - near_max), axis=3)

    def stat_step(running, key_block):
        old_max, old_sum = running
        scores = inner_dot(query_rows, key_block) * score_scale
        new_max = jnp.maximum(old_max, jnp.max(scores, axis=1))
        new_sum = old_sum * jnp.exp(old_max - new_max) + jnp.sum(
            jnp.exp(scores - new_max[:, None]), axis=1
        )
        return ((new_max, new_sum), None)

    stats, unused = lax.scan(
        stat_step, (near_max.reshape(row_total), near_sum.reshape(row_total)), key_blocks
    )
    log_total = stats[0] + jnp.log(stats[1])
    log_shaped = log_total.reshape(roll_local, seq_len, group_size, 1)
    near_probs = jnp.where(causal, jnp.exp(near_scores - log_shaped), 0.0).astype(jnp.bfloat16)
    near_output = jnp.einsum(
        "rsht,rtd->rshd", near_probs, value_head, preferred_element_type=jnp.float32
    ).reshape(row_total, head_width)

    def output_step(total_out, blocks):
        scores = inner_dot(query_rows, blocks[0]) * score_scale
        attn_probs = jnp.exp(scores - log_total[:, None]).astype(jnp.bfloat16)
        return (
            total_out + jnp.dot(attn_probs, blocks[1], preferred_element_type=jnp.float32),
            None,
        )

    output, unused = lax.scan(output_step, near_output, (key_blocks, value_blocks))
    row_delta = jnp.sum(grad_rows.astype(jnp.float32) * output, axis=1)
    context = (query_rows, grad_rows, log_total, row_delta, score_scale)
    contexts = [context]
    near_prob_grad = jnp.einsum(
        "rshd,rtd->rsht", grad_head, value_head, preferred_element_type=jnp.float32
    )
    delta_shaped = row_delta.reshape(roll_local, seq_len, group_size, 1)
    near_grad = (
        near_probs.astype(jnp.float32) * (near_prob_grad - delta_shaped) * score_scale
    ).astype(jnp.bfloat16)
    near_query = jnp.einsum(
        "rsht,rtd->rshd", near_grad, key_head, preferred_element_type=jnp.float32
    )
    key_new_grad = jnp.einsum(
        "rsht,rshd->rtd", near_grad, query_head, preferred_element_type=jnp.float32
    )
    value_new_grad = jnp.einsum(
        "rsht,rshd->rtd", near_probs, grad_head, preferred_element_type=jnp.float32
    )
    zero_rows = jnp.zeros((row_total, head_width), jnp.float32)

    def query_step(total_grad, blocks):
        attn_probs, score_grad = block_grads(context, blocks[0], blocks[1])
        return (
            total_grad + jnp.dot(score_grad, blocks[0], preferred_element_type=jnp.float32),
            None,
        )

    far_query, unused = lax.scan(query_step, zero_rows, (key_blocks, value_blocks))
    query_grad = far_query.reshape(roll_local, seq_len, group_size, head_width) + near_query
    query_list = [rotate(query_grad, cos_four, sin_four, -1.0).astype(jnp.bfloat16)]
    key_list = [
        rotate(key_new_grad, cos_four[:, :, 0], sin_four[:, :, 0], -1.0).astype(jnp.bfloat16)
    ]
    value_list = [value_new_grad.astype(jnp.bfloat16)]
    head_index = 0
    key_rows = cached_keys[:, head_index]
    value_rows = cached_values[:, head_index]
    pieces = [prompt_terms(contexts[head_index], key_rows, value_rows)]
    reduced = lax.psum_scatter(
        jnp.stack(pieces, axis=1).astype(jnp.bfloat16), "roll", scatter_dimension=0, tiled=True
    ).astype(jnp.float32)
    grad_queries = jnp.stack(query_list, axis=2)
    grad_keys_new = jnp.stack(key_list, axis=2)
    grad_values_new = jnp.stack(value_list, axis=2)
    return (
        grad_queries,
        grad_keys_new,
        grad_values_new,
        reduced[:, :, 0].astype(jnp.bfloat16),
        reduced[:, :, 1].astype(jnp.bfloat16),
    )


def solution(mesh):
    placed = (
        P("roll", "kvh", None),
        P("kvh", None, None, None),
        P("roll", None, "kvh", None, None),
        P("roll", None, "kvh", None),
        P("roll", None, "kvh", None),
        P("roll", "kvh", None),
        P("roll", "kvh", None),
        P("roll"),
    )
    return jax.shard_map(
        local,
        mesh=mesh,
        in_specs=placed,
        out_specs=(
            P("roll", None, "kvh", None, None),
            P("roll", None, "kvh", None),
            P("roll", None, "kvh", None),
            P("roll", "kvh", None),
            P("roll", "kvh", None),
        ),
        check_vma=False,
    )
```

profile of v0, /device:TPU:0, one launch (start us, length us, event | category | flops | bytes accessed | tf_op | source)
XLA Modules:
  0.0 133.3 jit_solution(5835152332438345986)
XLA Ops:
  8.0 17.7 %all_gather.9 = bf16[2048,1,128]{2,0,1:T(8,128)(2,1)} all-gather(bf16[256,1,128]{2,0,1:T(8,128)(2,1)} %param.21), channel_id=1, replica_groups=mesh['roll'=8,'kvh'=4] {'roll'}, dimensions={0}, use_global_device_ids=true | all-gather | bytes 589824 | tf_op jit(solution)/shard_map/all_gather | solution.py:88
  32.4 7.5 %while.43 = (s32[]{:T(128)}, f32[1280]{0:T(1024)S(1)}, f32[1280]{0:T(1024)S(1)}, bf16[4,512,128]{2,1,0:T(8,128)(2,1)}, bf16[1280,128]{1,0:T(8,128)(2,1)S(1)}, /*index=5*/s32[]{:T(128)}) while((s32[]{:T(128)}, f32[1280]{0:T(1024)S(1)}, f32[1280]{0:T(1024)S(1)}, bf16[4,512,128]{2,1,0:T(8,128)(2,1)}, bf16[1280,128]{1,0:T(8,128)(2,1)S(1)}, ...), condition=%wide.region_5.6_spmd, body=%wide.region_2.5_spmd.sunk | while | flops 170396160 | bytes 5768273 | solution.py:128
  32.4 1.4 %fusion.141 = (f32[1280]{0:T(1024)S(1)}, f32[512,1280]{1,0:T(8,128)S(1)}) fusion(bf16[1280,128]{1,0:T(8,128)(2,1)S(1)} %get-tuple-element.458, bf16[4,512,128]{2,1,0:T(8,128)(2,1)} %get-tuple-element.457, s32[]{:T(128)S(6)} %copy.79), kind=kOutput, calls=%fused_computation.131.clone.1 | convolution fusion | flops 169081600 | bytes 3085316 | tf_op jit(solution)/shard_map/while/body/eval_jaxpr/dot_general | solution.py:32
  34.3 1.4 %fusion.141 = (f32[1280]{0:T(1024)S(1)}, f32[512,1280]{1,0:T(8,128)S(1)}) fusion(bf16[1280,128]{1,0:T(8,128)(2,1)S(1)} %get-tuple-element.458, bf16[4,512,128]{2,1,0:T(8,128)(2,1)} %get-tuple-element.457, s32[]{:T(128)S(6)} %copy.79), kind=kOutput, calls=%fused_computation.131.clone.1 | convolution fusion | flops 169081600 | bytes 3085316 | tf_op jit(solution)/shard_map/while/body/eval_jaxpr/dot_general | solution.py:32
  36.2 1.4 %fusion.141 = (f32[1280]{0:T(1024)S(1)}, f32[512,1280]{1,0:T(8,128)S(1)}) fusion(bf16[1280,128]{1,0:T(8,128)(2,1)S(1)} %get-tuple-element.458, bf16[4,512,128]{2,1,0:T(8,128)(2,1)} %get-tuple-element.457, s32[]{:T(128)S(6)} %copy.79), kind=kOutput, calls=%fused_computation.131.clone.1 | convolution fusion | flops 169081600 | bytes 3085316 | tf_op jit(solution)/shard_map/while/body/eval_jaxpr/dot_general | solution.py:32
  38.1 1.4 %fusion.141 = (f32[1280]{0:T(1024)S(1)}, f32[512,1280]{1,0:T(8,128)S(1)}) fusion(bf16[1280,128]{1,0:T(8,128)(2,1)S(1)} %get-tuple-element.458, bf16[4,512,128]{2,1,0:T(8,128)(2,1)} %get-tuple-element.457, s32[]{:T(128)S(6)} %copy.79), kind=kOutput, calls=%fused_computation.131.clone.1 | convolution fusion | flops 169081600 | bytes 3085316 | tf_op jit(solution)/shard_map/while/body/eval_jaxpr/dot_general | solution.py:32
  42.1 16.1 %all_gather.10 = bf16[2048,1,128]{2,0,1:T(8,128)(2,1)} all-gather(bf16[256,1,128]{2,0,1:T(8,128)(2,1)S(1)} %copy-done.14), channel_id=1, replica_groups=mesh['roll'=8,'kvh'=4] {'roll'}, dimensions={0}, use_global_device_ids=true | all-gather | bytes 589824 | tf_op jit(solution)/shard_map/all_gather | solution.py:89
  58.6 7.8 %while.44 = (s32[]{:T(128)}, f32[1280,128]{1,0:T(8,128)S(1)}, bf16[4,512,128]{2,1,0:T(8,128)(2,1)}, bf16[1280,128]{1,0:T(8,128)(2,1)S(1)}, f32[1280]{0:T(1024)S(1)}, /*index=5*/bf16[4,512,128]{2,1,0:T(8,128)(2,1)}, s32[]{:T(128)}) while((s32[]{:T(128)}, f32[1280,128]{1,0:T(8,128)S(1)}, bf16[4,512,128]{2,1,0:T(8,128)(2,1)}, ...), condition=%wide.region_7.8_spmd, body=%wide.region_6.7_spmd.sunk | while | flops 337674240 | bytes 1906773 | solution.py:146
  58.6 1.9 %convolution_add_fusion.5 = f32[1280,128]{1,0:T(8,128)S(1)} fusion(f32[1280,128]{1,0:T(8,128)S(1)} %get-tuple-element.468, bf16[1280,128]{1,0:T(8,128)(2,1)S(1)} %get-tuple-element.477, f32[1280]{0:T(1024)S(1)} %get-tuple-element.478, bf16[4,512,128]{2,1,0:T(8,128)(2,1)} %get-tuple-element.479, s32[]{:T(128)S(6)} %copy.87, ...), kind=kOutput, calls=%fused_computation.10.clone.1 | convolution fusion | flops 337674240 | bytes 1906688 | tf_op jit(solution)/shard_map/while/body/eval_jaxpr/dot_general | solution.py:142
  60.5 1.9 %convolution_add_fusion.5 = f32[1280,128]{1,0:T(8,128)S(1)} fusion(f32[1280,128]{1,0:T(8,128)S(1)} %get-tuple-element.468, bf16[1280,128]{1,0:T(8,128)(2,1)S(1)} %get-tuple-element.477, f32[1280]{0:T(1024)S(1)} %get-tuple-element.478, bf16[4,512,128]{2,1,0:T(8,128)(2,1)} %get-tuple-element.479, s32[]{:T(128)S(6)} %copy.87, ...), kind=kOutput, calls=%fused_computation.10.clone.1 | convolution fusion | flops 337674240 | bytes 1906688 | tf_op jit(solution)/shard_map/while/body/eval_jaxpr/dot_general | solution.py:142
  62.5 1.9 %convolution_add_fusion.5 = f32[1280,128]{1,0:T(8,128)S(1)} fusion(f32[1280,128]{1,0:T(8,128)S(1)} %get-tuple-element.468, bf16[1280,128]{1,0:T(8,128)(2,1)S(1)} %get-tuple-element.477, f32[1280]{0:T(1024)S(1)} %get-tuple-element.478, bf16[4,512,128]{2,1,0:T(8,128)(2,1)} %get-tuple-element.479, s32[]{:T(128)S(6)} %copy.87, ...), kind=kOutput, calls=%fused_computation.10.clone.1 | convolution fusion | flops 337674240 | bytes 1906688 | tf_op jit(solution)/shard_map/while/body/eval_jaxpr/dot_general | solution.py:142
  64.4 1.9 %convolution_add_fusion.5 = f32[1280,128]{1,0:T(8,128)S(1)} fusion(f32[1280,128]{1,0:T(8,128)S(1)} %get-tuple-element.468, bf16[1280,128]{1,0:T(8,128)(2,1)S(1)} %get-tuple-element.477, f32[1280]{0:T(1024)S(1)} %get-tuple-element.478, bf16[4,512,128]{2,1,0:T(8,128)(2,1)} %get-tuple-element.479, s32[]{:T(128)S(6)} %copy.87, ...), kind=kOutput, calls=%fused_computation.10.clone.1 | convolution fusion | flops 337674240 | bytes 1906688 | tf_op jit(solution)/shard_map/while/body/eval_jaxpr/dot_general | solution.py:142
  66.4 5.9 %fusion.67 = bf16[256,5,128]{2,0,1:T(8,128)(2,1)S(1)} fusion(bf16[1,5,128,5120]{3,2,1,0:T(8,128)(2,1)} %param.17, bf16[1,256,5120]{2,1,0:T(8,128)(2,1)} %all-gather.2.cloned.1.call-done), kind=kOutput, calls=%fused_computation.75 | convolution fusion | flops 1677885440 | bytes 9502720 | tf_op jit(solution)/shard_map/rsc,ghdc->rsghd/dot_general | solution.py:81
  74.2 15.7 %while.45 = (s32[]{:T(128)}, bf16[4,512,2,128]{3,1,2,0:T(8,128)(2,1)S(1)}, bf16[4,512,128]{2,1,0:T(8,128)(2,1)}, bf16[1280,128]{1,0:T(8,128)(2,1)S(1)}, f32[1280...) while((s32[]{:T(128)}, ...), condition=%wide.region_12.13_spmd, body=%wide.region_11.12_spmd.sunk | while | flops 676855808 | bytes 6301809 | solution.py:69
  74.2 1.5 %fusion.152 = bf16[512,1280]{1,0:T(8,128)(2,1)S(1)} fusion(bf16[1280,128]{1,0:T(8,128)(2,1)S(1)} %get-tuple-element.532, f32[1280]{0:T(1024)S(1)} %get-tuple-element.533, bf16[4,512,128]{2,1,0:T(8,128)(2,1)} %get-tuple-element.531, s32[]{:T(128)S(6)} %copy.99), kind=kOutput, calls=%fused_computation.25.clone.1 | convolution fusion | flops 169738240 | bytes 1774596 | tf_op jit(solution)/shard_map/while/body/eval_jaxpr/dot_general | solution.py:32
  76.2 1.9 %fusion.153 = bf16[512,1,128]{2,0,1:T(8,128)(2,1)S(1)} fusion(bf16[1280,128]{1,0:T(8,128)(2,1)S(1)} %get-tuple-element.532, bf16[1280,128]{1,0:T(8,128)(2,1)S(1)} %get-tuple-element.535, bf16[512,1280]{1,0:T(8,128)(2,1)S(1)} %fusion.152, f32[1280]{0:T(1024)S(1)} %get-tuple-element.536, bf16[4,512,128]{2,1,0:T(8,128)(2,1)} %get-tuple-element.534, ...), kind=kOutput, calls=%fused_computation.30.clone.1 | convolution fusion | flops 338821120 | bytes 2233348 | tf_op jit(solution)/shard_map/while/body/eval_jaxpr/dot_general | solution.py:38
  78.2 1.5 %fusion.152 = bf16[512,1280]{1,0:T(8,128)(2,1)S(1)} fusion(bf16[1280,128]{1,0:T(8,128)(2,1)S(1)} %get-tuple-element.532, f32[1280]{0:T(1024)S(1)} %get-tuple-element.533, bf16[4,512,128]{2,1,0:T(8,128)(2,1)} %get-tuple-element.531, s32[]{:T(128)S(6)} %copy.99), kind=kOutput, calls=%fused_computation.25.clone.1 | convolution fusion | flops 169738240 | bytes 1774596 | tf_op jit(solution)/shard_map/while/body/eval_jaxpr/dot_general | solution.py:32
  80.2 1.9 %fusion.153 = bf16[512,1,128]{2,0,1:T(8,128)(2,1)S(1)} fusion(bf16[1280,128]{1,0:T(8,128)(2,1)S(1)} %get-tuple-element.532, bf16[1280,128]{1,0:T(8,128)(2,1)S(1)} %get-tuple-element.535, bf16[512,1280]{1,0:T(8,128)(2,1)S(1)} %fusion.152, f32[1280]{0:T(1024)S(1)} %get-tuple-element.536, bf16[4,512,128]{2,1,0:T(8,128)(2,1)} %get-tuple-element.534, ...), kind=kOutput, calls=%fused_computation.30.clone.1 | convolution fusion | flops 338821120 | bytes 2233348 | tf_op jit(solution)/shard_map/while/body/eval_jaxpr/dot_general | solution.py:38
  82.1 1.5 %fusion.152 = bf16[512,1280]{1,0:T(8,128)(2,1)S(1)} fusion(bf16[1280,128]{1,0:T(8,128)(2,1)S(1)} %get-tuple-element.532, f32[1280]{0:T(1024)S(1)} %get-tuple-element.533, bf16[4,512,128]{2,1,0:T(8,128)(2,1)} %get-tuple-element.531, s32[]{:T(128)S(6)} %copy.99), kind=kOutput, calls=%fused_computation.25.clone.1 | convolution fusion | flops 169738240 | bytes 1774596 | tf_op jit(solution)/shard_map/while/body/eval_jaxpr/dot_general | solution.py:32
  84.1 1.9 %fusion.153 = bf16[512,1,128]{2,0,1:T(8,128)(2,1)S(1)} fusion(bf16[1280,128]{1,0:T(8,128)(2,1)S(1)} %get-tuple-element.532, bf16[1280,128]{1,0:T(8,128)(2,1)S(1)} %get-tuple-element.535, bf16[512,1280]{1,0:T(8,128)(2,1)S(1)} %fusion.152, f32[1280]{0:T(1024)S(1)} %get-tuple-element.536, bf16[4,512,128]{2,1,0:T(8,128)(2,1)} %get-tuple-element.534, ...), kind=kOutput, calls=%fused_computation.30.clone.1 | convolution fusion | flops 338821120 | bytes 2233348 | tf_op jit(solution)/shard_map/while/body/eval_jaxpr/dot_general | solution.py:38
  86.1 1.5 %fusion.152 = bf16[512,1280]{1,0:T(8,128)(2,1)S(1)} fusion(bf16[1280,128]{1,0:T(8,128)(2,1)S(1)} %get-tuple-element.532, f32[1280]{0:T(1024)S(1)} %get-tuple-element.533, bf16[4,512,128]{2,1,0:T(8,128)(2,1)} %get-tuple-element.531, s32[]{:T(128)S(6)} %copy.99), kind=kOutput, calls=%fused_computation.25.clone.1 | convolution fusion | flops 169738240 | bytes 1774596 | tf_op jit(solution)/shard_map/while/body/eval_jaxpr/dot_general | solution.py:32
  88.1 1.9 %fusion.153 = bf16[512,1,128]{2,0,1:T(8,128)(2,1)S(1)} fusion(bf16[1280,128]{1,0:T(8,128)(2,1)S(1)} %get-tuple-element.532, bf16[1280,128]{1,0:T(8,128)(2,1)S(1)} %get-tuple-element.535, bf16[512,1280]{1,0:T(8,128)(2,1)S(1)} %fusion.152, f32[1280]{0:T(1024)S(1)} %get-tuple-element.536, bf16[4,512,128]{2,1,0:T(8,128)(2,1)} %get-tuple-element.534, ...), kind=kOutput, calls=%fused_computation.30.clone.1 | convolution fusion | flops 338821120 | bytes 2233348 | tf_op jit(solution)/shard_map/while/body/eval_jaxpr/dot_general | solution.py:38
  91.1 17.3 %while.46 = (s32[]{:T(128)}, f32[1280,128]{1,0:T(8,128)}, bf16[4,512,128]{2,1,0:T(8,128)(2,1)}, bf16[1280,128]{1,0:T(8,128)(2,1)S(1)}, f32[1280]{0:T(1024)S(1)},...) while((s32[]{:T(128)}, f32[1280,128]{1,0:T(8,128)}, ...), condition=%wide.region_10.11_spmd.clone, body=%wide.region_9.10_spmd.clone.sunk | while | flops 508887040 | bytes 7614074 | solution.py:175
  91.1 1.4 %fusion.160 = f32[512,1280]{1,0:T(8,128)S(1)} fusion(bf16[1280,128]{1,0:T(8,128)(2,1)S(1)} %get-tuple-element.504, f32[1280]{0:T(1024)S(1)} %get-tuple-element.505, bf16[4,512,128]{2,1,0:T(8,128)(2,1)} %get-tuple-element.503, s32[]{:T(128)S(6)} %copy.93), kind=kOutput, calls=%fused_computation.48.clone.1 | convolution fusion | flops 170393600 | bytes 3085316 | tf_op jit(solution)/shard_map/while/body/eval_jaxpr/dot_general | solution.py:32
  92.5 2.7 %convolution_add_fusion.6 = f32[1280,128]{1,0:T(8,128)} fusion(f32[512,1280]{1,0:T(8,128)S(1)} %fusion.160, bf16[1280,128]{1,0:T(8,128)(2,1)S(1)} %get-tuple-element.507, f32[1280]{0:T(1024)S(1)} %get-tuple-element.508, f32[1280,128]{1,0:T(8,128)} %get-tuple-element.492, pred[]{:T(512)S(6)} %compare.3, bf16[4,512,128]{2,1,0:T(8,128)(2,1)} %get-tuple-element.506, ...), kind=kOutput, calls=%fused_computation.50.clone.1 | convolution fusion | flops 338493440 | bytes 4528640 | tf_op jit(solution)/shard_map/while/body/eval_jaxpr/dot_general | solution.py:171
  96.6 2.9 %convolution_add_fusion.6 = f32[1280,128]{1,0:T(8,128)} fusion(f32[512,1280]{1,0:T(8,128)S(1)} %fusion.160, bf16[1280,128]{1,0:T(8,128)(2,1)S(1)} %get-tuple-element.507, f32[1280]{0:T(1024)S(1)} %get-tuple-element.508, f32[1280,128]{1,0:T(8,128)} %get-tuple-element.492, pred[]{:T(512)S(6)} %compare.3, bf16[4,512,128]{2,1,0:T(8,128)(2,1)} %get-tuple-element.506, ...), kind=kOutput, calls=%fused_computation.50.clone.1 | convolution fusion | flops 338493440 | bytes 4528640 | tf_op jit(solution)/shard_map/while/body/eval_jaxpr/dot_general | solution.py:171
  99.6 1.4 %fusion.160 = f32[512,1280]{1,0:T(8,128)S(1)} fusion(bf16[1280,128]{1,0:T(8,128)(2,1)S(1)} %get-tuple-element.504, f32[1280]{0:T(1024)S(1)} %get-tuple-element.505, bf16[4,512,128]{2,1,0:T(8,128)(2,1)} %get-tuple-element.503, s32[]{:T(128)S(6)} %copy.93), kind=kOutput, calls=%fused_computation.48.clone.1 | convolution fusion | flops 170393600 | bytes 3085316 | tf_op jit(solution)/shard_map/while/body/eval_jaxpr/dot_general | solution.py:32
  101.0 2.9 %convolution_add_fusion.6 = f32[1280,128]{1,0:T(8,128)} fusion(f32[512,1280]{1,0:T(8,128)S(1)} %fusion.160, bf16[1280,128]{1,0:T(8,128)(2,1)S(1)} %get-tuple-element.507, f32[1280]{0:T(1024)S(1)} %get-tuple-element.508, f32[1280,128]{1,0:T(8,128)} %get-tuple-element.492, pred[]{:T(512)S(6)} %compare.3, bf16[4,512,128]{2,1,0:T(8,128)(2,1)} %get-tuple-element.506, ...), kind=kOutput, calls=%fused_computation.50.clone.1 | convolution fusion | flops 338493440 | bytes 4528640 | tf_op jit(solution)/shard_map/while/body/eval_jaxpr/dot_general | solution.py:171
  103.9 1.4 %fusion.160 = f32[512,1280]{1,0:T(8,128)S(1)} fusion(bf16[1280,128]{1,0:T(8,128)(2,1)S(1)} %get-tuple-element.504, f32[1280]{0:T(1024)S(1)} %get-tuple-element.505, bf16[4,512,128]{2,1,0:T(8,128)(2,1)} %get-tuple-element.503, s32[]{:T(128)S(6)} %copy.93), kind=kOutput, calls=%fused_computation.48.clone.1 | convolution fusion | flops 170393600 | bytes 3085316 | tf_op jit(solution)/shard_map/while/body/eval_jaxpr/dot_general | solution.py:32
  105.4 2.9 %convolution_add_fusion.6 = f32[1280,128]{1,0:T(8,128)} fusion(f32[512,1280]{1,0:T(8,128)S(1)} %fusion.160, bf16[1280,128]{1,0:T(8,128)(2,1)S(1)} %get-tuple-element.507, f32[1280]{0:T(1024)S(1)} %get-tuple-element.508, f32[1280,128]{1,0:T(8,128)} %get-tuple-element.492, pred[]{:T(512)S(6)} %compare.3, bf16[4,512,128]{2,1,0:T(8,128)(2,1)} %get-tuple-element.506, ...), kind=kOutput, calls=%fused_computation.50.clone.1 | convolution fusion | flops 338493440 | bytes 4528640 | tf_op jit(solution)/shard_map/while/body/eval_jaxpr/dot_general | solution.py:171
  114.7 10.2 %reduce-scatter.2.cloned.1.call-done = bf16[256,1,2,128]{3,0,2,1:T(8,128)(2,1)} async-done(((bf16[2048,1,2,128]{3,0,2,1:T(8,128)(2,1)}), bf16[256,1,2,128]{3,0,2,1:T(8,128)(2,1)}) %reduce-scatter.2.cloned.1.call-update) | async-done | bytes 131088 | tf_op jit(solution)/shard_map/reduce_scatter | solution.py:186
  124.9 1.5 %slice_bitcast_fusion = (bf16[256,1,128]{2,0,1:T(8,128)(2,1)}, bf16[256,1,128]{2,0,1:T(8,128)(2,1)}) fusion(bf16[256,1,2,128]{3,0,2,1:T(8,128)(2,1)} %reduce-scatter.2.cloned.1.call-done), kind=kLoop, calls=%fused_computation.113 | loop fusion | bytes 262144 | tf_op jit(solution)/shard_map/convert_element_type | solution.py:197
  (108 shorter events, 23.7 us)
Async XLA Ops:
  7.2 51.1 %copy-start = (bf16[1,256,1,128]{3,1,2,0:T(8,128)(2,1)S(1)}, bf16[1,256,1,128]{3,1,2,0:T(8,128)(2,1)}, u32[]{:S(2)}) copy-start(bf16[1,256,1,128]{3,1,2,0:T(8,128)(2,1)} %param.20) | copy-start | bytes 196612
  7.2 59.2 %all-gather.2.cloned.1.call-start = ((), (), s32[]{:S(2)}) async-start(), calls=%async_computation.1 | async-start | bytes 3276800 | tf_op jit(solution)/shard_map/all_gather | solution.py:83
  7.9 117.0 %reduce-scatter.2.cloned.1.call-start = ((), (), s32[]{:S(2)}) async-start(), calls=%async_computation.2 | async-start | bytes 1179648 | tf_op jit(solution)/shard_map/reduce_scatter | solution.py:186
  28.6 1.3 copy-start.13
  28.9 2.1 %copy-start.3 = (bf16[1,256,1,5,64]{4,1,3,2,0:T(8,128)(2,1)}, bf16[1,256,1,5,64]{4,1,3,2,0:T(8,128)(2,1)S(1)}, u32[]{:S(2)}) copy-start(bf16[1,256,1,5,64]{4,1,3,2,0:T(8,128)(2,1)S(1)} %get-tuple-element.257) | copy-start | bytes 491524
  28.9 2.1 %copy-start.5 = (bf16[1,256,1,5,64]{4,1,3,2,0:T(8,128)(2,1)}, bf16[1,256,1,5,64]{4,1,3,2,0:T(8,128)(2,1)S(1)}, u32[]{:S(2)}) copy-start(bf16[1,256,1,5,64]{4,1,3,2,0:T(8,128)(2,1)S(1)} %get-tuple-element.258) | copy-start | bytes 491524
  30.5 1.6 %copy-start.10 = (bf16[256,64]{1,0:T(8,128)(2,1)}, bf16[256,64]{1,0:T(8,128)(2,1)S(1)}, u32[]{:S(2)}) copy-start(bf16[256,64]{1,0:T(8,128)(2,1)S(1)} %get-tuple-element.264) | copy-start | bytes 98308
  40.3 1.9 %copy-start.14 = (bf16[256,1,128]{2,0,1:T(8,128)(2,1)S(1)}, bf16[256,1,128]{2,0,1:T(8,128)(2,1)}, u32[]{:S(2)}) copy-start(bf16[256,1,128]{2,0,1:T(8,128)(2,1)} %param.22) | copy-start | bytes 196612
  40.6 0.9 copy-start.1
  72.3 0.7 copy-start.7
  73.0 1.2 copy-start.9
  108.3 1.9 %copy-start.2 = (bf16[256,5,256]{2,0,1:T(8,128)(2,1)S(1)}, bf16[256,5,256]{2,0,1:T(8,128)(2,1)}, u32[]{:S(2)}) copy-start(bf16[256,5,256]{2,0,1:T(8,128)(2,1)} %copy-done.1) | copy-start | bytes 1966084
  108.3 1.9 %copy-start.8 = (bf16[256,5,128]{2,0,1:T(8,128)(2,1)S(1)}, bf16[256,5,128]{2,0,1:T(8,128)(2,1)}, u32[]{:S(2)}) copy-start(bf16[256,5,128]{2,0,1:T(8,128)(2,1)} %copy-done.7) | copy-start | bytes 983044
  108.5 2.1 %copy-start.11 = (bf16[256,64]{1,0:T(8,128)(2,1)S(1)}, bf16[256,64]{1,0:T(8,128)(2,1)}, u32[]{:S(2)}) copy-start(bf16[256,64]{1,0:T(8,128)(2,1)} %copy-done.10) | copy-start | bytes 98308
  109.8 1.3 copy-start.12
  110.6 1.5 %copy-start.4 = (bf16[1,256,1,5,64]{4,1,3,2,0:T(8,128)(2,1)S(1)}, bf16[1,256,1,5,64]{4,1,3,2,0:T(8,128)(2,1)}, u32[]{:S(2)}) copy-start(bf16[1,256,1,5,64]{4,1,3,2,0:T(8,128)(2,1)} %copy-done.3) | copy-start | bytes 491524
  110.6 1.5 %copy-start.6 = (bf16[1,256,1,5,64]{4,1,3,2,0:T(8,128)(2,1)S(1)}, bf16[1,256,1,5,64]{4,1,3,2,0:T(8,128)(2,1)}, u32[]{:S(2)}) copy-start(bf16[1,256,1,5,64]{4,1,3,2,0:T(8,128)(2,1)} %copy-done.5) | copy-start | bytes 491524
Sparse Core Ops, SparseCore 0:
  9.8 42.2 all-gather.1
  91.2 33.7 reduce-scatter.1
where the time goes:
time: 134 us; the launch traced here: 133 us
  matrix products  55.1 us (41%)
  blocking collectives  33.9 us (25%)
  between operations  15.1 us (11%)
  local copies, waits for them, and re-layouts  11.4 us (9%)
  waiting for transfers between devices  11 us (8%)
  other arithmetic  6.39 us (5%)
    all_gather x1, blocking collectives, local(): lax.all_gather(keys_prompt, 'roll', axis=0, tiled=True)  17.7 us
    dot_general x12, matrix products, inner_dot(): lax.dot_general(left, right, (((1,), (1,)), ((), ())), preferred_element_...  17.3 us
    all_gather x1, blocking collectives, local(): lax.all_gather(values_prompt, 'roll', axis=0, tiled=True)  16.1 us
    dot_general x4, matrix products, query_step(): jnp.dot(score_grad, blocks[0], preferred_element_type=jnp.float32)  11.5 us
    reduce_scatter x1, waiting for transfers between devices, local(): lax.psum_scatter(jnp.stack(pieces, axis=1).astype(jnp.bfloat16), 'roll',...  10.2 us
    dot_general x8, matrix products, outer_sum(): lax.dot_general(left, right, (((0,), (0,)), ((), ())), preferred_element_...  9.5 us
    dot_general x4, matrix products, output_step(): jnp.dot(attn_probs, blocks[1], preferred_element_type=jnp.float32)  7.7 us
    dot_general x1, matrix products, local(): jnp.einsum('rsc,ghdc->rsghd', lax.all_gather(out_grad, 'kvh', axis=1, til...  5.89 us
  transfers between devices with their start and end apart: 2, of which 1 were waited for; matrix products, arithmetic and copies ran while one was open for 34% of the time, Pallas kernels for 0%

commit v1 on v0

v1 whole, which is shorter than its diff:
```python
import functools
import math

import jax
import jax.numpy as jnp
from jax import lax
from jax.experimental import pallas as pl
from jax.experimental.pallas import tpu as pltpu
from jax.sharding import PartitionSpec as P


theta_base = 1000000.0
f32 = jnp.float32
bf16 = jnp.bfloat16


def flip(value, axis_name, mask):
    count = lax.axis_size(axis_name)
    return lax.ppermute(value, axis_name, [(i, i ^ mask) for i in range(count)])


def rope_tables(positions, head_width):
    half_width = head_width // 2
    frequency = jnp.power(theta_base, -(jnp.arange(half_width, dtype=f32) / half_width))
    angles = positions.astype(f32)[:, None] * frequency[None, :]
    cos_part, sin_part = jnp.cos(angles), jnp.sin(angles)
    return (
        jnp.concatenate([cos_part, cos_part], axis=1),
        jnp.concatenate([-sin_part, sin_part], axis=1),
    )


def turn(rows, cos_full, sin_full):
    return rows * cos_full + pltpu.roll(rows, rows.shape[1] // 2, 1) * sin_full


def dot(left, right):
    return jnp.dot(left, right, preferred_element_type=f32)


def fold_rows(block, op):
    return op(block.reshape(block.shape[0] // 8, 8, block.shape[1]), axis=0)


def local_call(kernel, out_shape, flops, scratch_shapes=(), in_specs=None, **kwargs):
    return pl.pallas_call(
        kernel,
        out_shape=out_shape,
        in_specs=in_specs,
        out_specs=jax.tree.map(lambda _: vmem, out_shape),
        scratch_shapes=scratch_shapes,
        compiler_params=pltpu.CompilerParams(vmem_limit_bytes=vmem_grant),
        cost_estimate=pl.CostEstimate(flops=flops, bytes_accessed=flops // 512, transcendentals=0),
        **kwargs,
    )


vmem = pl.BlockSpec(memory_space=pltpu.VMEM)
vmem_grant = 24 << 20


def probability_kernel(scale, count, groups, *refs):
    q_ref, kn_ref, vn_ref, cos_ref, sin_ref = refs[:5]
    chunk_refs = refs[5 : 5 + count]
    p_refs = refs[5 + count : 5 + count + len(groups)]
    qr_ref, near_ref, o_ref, s_scr, vt_scr, chunk_scr, sems = refs[5 + count + len(groups) :]
    heads, seq, _ = q_ref.shape
    copies = [
        pltpu.make_async_copy(ref, chunk_scr.at[c], sems.at[c]) for c, ref in enumerate(chunk_refs)
    ]
    for copy in copies:
        copy.start()
    factor = scale * math.log2(math.e)
    near_ref[0] = turn(kn_ref[...].astype(f32), cos_ref[...], sin_ref[...]).astype(bf16)
    near_ref[1] = vn_ref[...]
    chunks = [near_ref] + [chunk_scr.at[c] for c in range(count)]
    goals = {}
    for p_ref, group in zip(p_refs, groups):
        for j, c in enumerate(group):
            goals[c] = p_ref.at[j]
    q_cols = []
    for h in range(heads):
        q_rows = turn(q_ref[h].astype(f32), cos_ref[...], sin_ref[...])
        qr_ref[h] = q_rows.astype(bf16)
        q_cols.append(q_rows.T.astype(bf16))
    tops, masses, outs = {}, {}, {}
    waited = set()
    for t in range(heads + 2):
        for c in range(count + 1):
            if c > 0 and c not in waited:
                copies[c - 1].wait()
                waited.add(c)
            if t == 0:
                vt_scr[c] = chunks[c][1].astype(f32).T.astype(bf16)
            if t < heads:
                s = dot(chunks[c][0], q_cols[t])
                if c == 0:
                    key_at = lax.broadcasted_iota(jnp.int32, s.shape, 0)
                    row_at = lax.broadcasted_iota(jnp.int32, s.shape, 1)
                    s = jnp.where(key_at <= row_at, s, -jnp.inf)
                s_scr[t % 3, c] = s
                top = fold_rows(s, jnp.max)
                tops[t] = jnp.maximum(tops[t], top) if c else top
            if 0 <= t - 1 < heads:
                h = t - 1
                if c == 0:
                    tops[h] = jnp.max(tops[h], axis=0, keepdims=True)
                e = jnp.exp2((s_scr[h % 3, c] - tops[h]) * factor)
                s_scr[h % 3, c] = e
                mass = fold_rows(e, jnp.sum)
                masses[h] = masses[h] + mass if c else mass
            if 0 <= t - 2:
                h = t - 2
                cols = slice(h * seq, (h + 1) * seq)
                if c == 0:
                    masses[h] = 1.0 / jnp.sum(masses[h], axis=0, keepdims=True)
                probs = (s_scr[h % 3, c] * masses[h]).astype(bf16)
                goals[c][:, cols] = probs
                out = dot(vt_scr[c], probs)
                outs[h] = outs[h] + out if c else out
                if c == count:
                    o_ref[:, cols] = outs[h]


def project_kernel(count, slots_ref, *refs):
    w_ref, o_ref = refs[count : count + 2]
    g_ref, gt_ref, delta_ref, og_scr = refs[count + 2 :]
    for i, ref in enumerate(refs[:count]):
        rows = ref.shape[0]
        og_scr[pl.ds(pl.multiple_of(slots_ref[i] * rows, rows), rows), :] = ref[...]
    heads, seq, width = g_ref.shape
    for h in range(heads):
        cols = slice(h * seq, (h + 1) * seq)
        rows = lax.dot_general(
            w_ref[h * width : (h + 1) * width, :],
            og_scr[...],
            (((1,), (1,)), ((), ())),
            preferred_element_type=f32,
        ).astype(bf16)
        gt_ref[:, cols] = rows
        g_ref[h] = rows.astype(f32).T.astype(bf16)
        delta_ref[:, cols] = jnp.sum(rows.astype(f32) * o_ref[:, cols], axis=0, keepdims=True)


def project_call(slots, pieces, weight, o, heads):
    outs, depth = weight.shape
    width = outs // heads
    seq = sum(piece.shape[0] for piece in pieces)
    return local_call(
        functools.partial(project_kernel, len(pieces)),
        [
            jax.ShapeDtypeStruct((heads, seq, width), bf16),
            jax.ShapeDtypeStruct((width, heads * seq), bf16),
            jax.ShapeDtypeStruct((1, heads * seq), f32),
        ],
        2 * outs * seq * depth,
        in_specs=[pl.BlockSpec(memory_space=pltpu.SMEM)] + [vmem] * (len(pieces) + 2),
        scratch_shapes=[pltpu.VMEM((seq, depth), bf16)],
    )(slots, *pieces, weight, o)


def chunk_gradients(scale, p_ref, keys, values, q_ref, g_ref, gt_ref, delta_ref, add_dq):
    heads, seq, _ = q_ref.shape
    keys_t = keys.astype(f32).T.astype(bf16)
    dk = dv = None
    for h in range(heads):
        cols = slice(h * seq, (h + 1) * seq)
        p = p_ref[:, cols]
        dp = dot(values, gt_ref[:, cols])
        ds = (p.astype(f32) * (dp - delta_ref[:, cols]) * scale).astype(bf16)
        dv_h = dot(p, g_ref[h])
        dk_h = dot(ds, q_ref[h])
        dk, dv = (dk_h, dv_h) if dk is None else (dk + dk_h, dv + dv_h)
        add_dq(cols, dot(keys_t, ds))
    return dk, dv


def gradient_kernel(scale, count, got_at, is_last, split, *refs):
    it = iter(refs)
    take = lambda n: [next(it) for _ in range(n)]
    p_ref, q_ref, g_ref, gt_ref, delta_ref = take(5)
    chunk_refs = take(count)
    got_ref = next(it) if got_at is not None else None
    if is_last:
        near_ref, cos_ref, sin_ref, *dq_refs = take(7)
    out_refs = take(count if split else 1)
    if is_last:
        near_out, dq_out = take(2)
    dq_acc = next(it)
    started = []

    def add_dq(cols, term):
        if cols.start in started:
            dq_acc[:, cols] += term
        else:
            started.append(cols.start)
            dq_acc[:, cols] = term

    first = 1 if is_last else 0
    common = (q_ref, g_ref, gt_ref, delta_ref, add_dq)
    if is_last:
        dk, dv = chunk_gradients(scale, p_ref.at[0], near_ref[0], near_ref[1], *common)
        near_out[0] = turn(dk, cos_ref[...], -sin_ref[...]).astype(bf16)
        near_out[1] = dv.astype(bf16)
    for j, chunk in enumerate(chunk_refs):
        dk, dv = chunk_gradients(scale, p_ref.at[first + j], chunk[0], chunk[1], *common)
        if got_at is not None:
            dk = dk + got_ref[got_at + j, 0].astype(f32)
            dv = dv + got_ref[got_at + j, 1].astype(f32)
        to = out_refs[j] if split else out_refs[0].at[j]
        to[0] = dk.astype(to.dtype)
        to[1] = dv.astype(to.dtype)
    if is_last:
        heads, seq, _ = q_ref.shape
        for h in range(heads):
            cols = slice(h * seq, (h + 1) * seq)
            total = dq_acc[:, cols]
            for ref in dq_refs:
                total = total + ref[:, cols]
            dq_out[h] = turn(total.T, cos_ref[...], -sin_ref[...]).astype(bf16)


def gradient_call(scale, p, common, chunks, got=None, got_at=None, last=None, kinds=None):
    q = common[0]
    heads, seq, width = q.shape
    count = len(chunks)
    shape = chunks[0].shape
    if kinds is None:
        out_shape = [jax.ShapeDtypeStruct((count, *shape), bf16)]
    else:
        out_shape = [jax.ShapeDtypeStruct(shape, kind) for kind in kinds]
    operands = [p, *common, *chunks] + ([got] if got is not None else []) + list(last or ())
    dq_shape = (width, heads * seq)
    scratch = []
    if last:
        out_shape += [jax.ShapeDtypeStruct(shape, bf16), jax.ShapeDtypeStruct(q.shape, bf16)]
        scratch = [pltpu.VMEM(dq_shape, f32)]
    else:
        out_shape += [jax.ShapeDtypeStruct(dq_shape, f32)]
    return local_call(
        functools.partial(
            gradient_kernel, scale, count, got_at, bool(last), kinds is not None
        ),
        out_shape,
        8 * heads * seq * p.shape[0] * p.shape[1] * width,
        in_specs=[vmem] * len(operands),
        scratch_shapes=scratch,
    )(*operands)


def gather_pieces(own):
    rolls, count = lax.axis_size("roll"), lax.axis_size("kvh")
    bits = count.bit_length() - 1
    if count != 1 << bits:
        raise ValueError("unsupported mesh")
    turned = lambda mask, core: sum(
        1 << ((k + core) % bits) for k in range(bits) if mask & (1 << k)
    )
    pieces = [own]
    for mask in range(1, count):
        high = 1 << (mask.bit_length() - 1)
        pairs = [
            (r * count + k, r * count + (k ^ turned(high, r % 2)))
            for r in range(rolls)
            for k in range(count)
        ]
        pieces.append(lax.ppermute(pieces[mask ^ high], ("roll", "kvh"), pairs))
    core = lax.axis_index("roll") % 2
    masks = [jnp.array([turned(m, c) for m in range(count)], jnp.int32) for c in range(2)]
    return pieces, lax.axis_index("kvh") ^ jnp.where(core == 0, *masks)


def body(out_grad, out_weight, queries, keys_new, values_new, keys_prompt, values_prompt, offsets):
    _, seq, _, heads, width = queries.shape
    roll_count = lax.axis_size("roll")
    chunk_len = keys_prompt.shape[0]
    prompt_total = chunk_len * roll_count
    scale = width ** (-0.5)
    chips = roll_count // 2
    if chips < 2 or chunk_len != seq:
        raise ValueError("unsupported mesh")
    far = list(range(chips - 1, 1, -1))
    shape = jax.ShapeDtypeStruct
    rows = heads * seq

    pieces, slots = gather_pieces(out_grad[0])
    even = {0: jnp.stack([keys_prompt[:, 0], values_prompt[:, 0]])}
    for m in far + [1]:
        even[m] = flip(even[0], "roll", 2 * m)
    odd = {}
    for m in [0, 1] + far:
        odd[m] = flip(even[m], "roll", 1)

    positions = prompt_total + offsets[0] + jnp.arange(seq, dtype=jnp.int32)
    cos_full, sin_full = rope_tables(positions, width)
    q = jnp.transpose(queries[0, :, 0], (1, 0, 2))
    chunks = [even[0], odd[0], even[1], odd[1]] + [even[m] for m in far] + [odd[m] for m in far]
    n = len(far)
    groups = (range(5 + n, 5 + 2 * n), range(5, 5 + n), (4, 2), (3,), (0, 1))
    *probs, q_rot, near, o = local_call(
        functools.partial(probability_kernel, scale, len(chunks), groups),
        [shape((len(group), seq, rows), bf16) for group in groups]
        + [shape(q.shape, bf16), shape((2, seq, width), bf16), shape((width, rows), f32)],
        4 * rows * (1 + len(chunks)) * seq * width,
        in_specs=[vmem] * 5 + [pl.BlockSpec(memory_space=pl.ANY)] * len(chunks),
        scratch_shapes=[
            pltpu.VMEM((3, len(chunks) + 1, seq, seq), f32),
            pltpu.VMEM((len(chunks) + 1, width, seq), bf16),
            pltpu.VMEM((len(chunks), 2, seq, width), bf16),
            pltpu.SemaphoreType.DMA((len(chunks),)),
        ],
    )(q, keys_new[0, :, 0], values_new[0, :, 0], cos_full, sin_full, *chunks)
    p_odd, p_even, p_close, p_one, p_near = probs

    g, gt, delta = project_call(
        slots, pieces, out_weight.reshape(heads * width, -1), o, heads
    )

    common = (q_rot, g, gt, delta)
    sums, dq1 = gradient_call(scale, p_odd, common, [odd[m] for m in far])
    got = flip(sums, "roll", 1)
    *sums, dq2 = gradient_call(
        scale, p_even, common, [even[m] for m in far], got, 0, kinds=[bf16] * len(far)
    )
    arrived = []
    for m, part in zip(far, sums):
        arrived.append(flip(part, "roll", 2 * m))
    sums, dq3 = gradient_call(scale, p_close, common, [odd[1], odd[0]])
    got = flip(sums, "roll", 1)
    part, dq4 = gradient_call(scale, p_one, common, [even[1]], got, 0, kinds=[bf16])
    arrived.append(flip(part, "roll", 2))
    total, near_grads, dq = gradient_call(
        scale, p_near, common, [even[0]], got, 1,
        last=(near, cos_full, sin_full, dq1, dq2, dq3, dq4), kinds=[f32],
    )
    for part in arrived:
        total = total + part.astype(f32)
    total = total.astype(bf16)
    return (
        jnp.transpose(dq, (1, 0, 2))[None, :, None],
        near_grads[0][None, :, None],
        near_grads[1][None, :, None],
        total[0][:, None],
        total[1][:, None],
    )


def solution(mesh):
    placed = (
        P("roll", "kvh", None),
        P("kvh", None, None, None),
        P("roll", None, "kvh", None, None),
        P("roll", None, "kvh", None),
        P("roll", None, "kvh", None),
        P("roll", "kvh", None),
        P("roll", "kvh", None),
        P("roll"),
    )
    return jax.shard_map(
        body,
        mesh=mesh,
        in_specs=placed,
        out_specs=(
            P("roll", None, "kvh", None, None),
            P("roll", None, "kvh", None),
            P("roll", None, "kvh", None),
            P("roll", "kvh", None),
            P("roll", "kvh", None),
        ),
        check_vma=False,
    )
```

time: 134 us -> 62.6 us (0.47)
  matrix products: 55.1 us -> 0 us
  blocking collectives: 33.9 us -> 0 us
  Pallas kernels: 0 us -> 23.5 us
  starting transfers between devices: 0.08 us -> 15.1 us
  between operations: 15.1 us -> 1.43 us
  local copies, waits for them, and re-layouts: 11.4 us -> 3.26 us
  waiting for transfers between devices: 11 us -> 17.5 us
  other arithmetic: 6.39 us -> 1.64 us
    dot_general x35 -> x0, matrix products: 55.1 us -> none  [the longest x12 17.3 us: inner_dot(): lax.dot_general(left, right, (((1,), (1,)), ((), ())), preferred_element_...]
    all_gather x2 -> x0, blocking collectives: 33.9 us -> none  [the longest x1 17.7 us: local(): lax.all_gather(keys_prompt, 'roll', axis=0, tiled=True)]
    pallas_call x0 -> x7, Pallas kernels: none -> 23.5 us  [the longest x5 10.9 us: gradient_call(): local_call(functools.partial(gradient_kernel, scale, count, got_at, bool(...]
    ppermute x0 -> x15, waiting for transfers between devices: none -> 17.5 us  [the longest x12 12.5 us: flip(): return lax.ppermute(value, axis_name, [(i, i ^ mask) for i in range(count)])]
    ppermute x0 -> x15, starting transfers between devices: none -> 15.1 us  [the longest x12 10 us: flip(): return lax.ppermute(value, axis_name, [(i, i ^ mask) for i in range(count)])]
    reduce_scatter x1 -> x0, waiting for transfers between devices: 10.2 us -> none  [local(): lax.psum_scatter(jnp.stack(pieces, axis=1).astype(jnp.bfloat16), 'roll',...]
    convert_element_type x4 -> x0, local copies, waits for them, and re-layouts: 3.23 us -> none  [the longest x1 1.53 us: local(): reduced[:, :, 1].astype(jnp.bfloat16)]
    reduce_sum x6 -> x0, other arithmetic: 2.32 us -> none  [the longest x4 1.62 us: stat_step(): jnp.sum(jnp.exp(scores - new_max[:, None]), axis=1)]
  transfers between devices with their start and end apart: 2 -> 15, of which waited for: 1 -> 6; matrix products, arithmetic and copies ran while one was open for 34% -> 4% of each run, Pallas kernels for 0% -> 26%
where the time goes in v1:
time: 62.6 us; the launch traced here: 62.4 us
  Pallas kernels  23.5 us (38%)
  waiting for transfers between devices  17.5 us (28%)
  starting transfers between devices  15.1 us (24%)
  local copies, waits for them, and re-layouts  3.26 us (5%)
  other arithmetic  1.64 us (3%)
  between operations  1.43 us (2%)
    ppermute x12, waiting for transfers between devices, flip(): return lax.ppermute(value, axis_name, [(i, i ^ mask) for i in range(count)])  12.5 us
    pallas_call x5, Pallas kernels, gradient_call(): local_call(functools.partial(gradient_kernel, scale, count, got_at, bool(...  10.9 us
    ppermute x12, starting transfers between devices, flip(): return lax.ppermute(value, axis_name, [(i, i ^ mask) for i in range(count)])  10 us
    pallas_call x1, Pallas kernels, body(): local_call(functools.partial(probability_kernel, scale, len(chunks), grou...  7.41 us
    pallas_call x1, Pallas kernels, project_call(): local_call(functools.partial(project_kernel, len(pieces)), [jax.ShapeDtyp...  5.14 us
    ppermute x3, starting transfers between devices, gather_pieces(): pieces.append(lax.ppermute(pieces[mask ^ high], ('roll', 'kvh'), pairs))  5.06 us
    ppermute x3, waiting for transfers between devices, gather_pieces(): pieces.append(lax.ppermute(pieces[mask ^ high], ('roll', 'kvh'), pairs))  5.03 us
    unnamed x10, local copies, waits for them, and re-layouts  1.94 us
  transfers between devices with their start and end apart: 15, of which 6 were waited for; matrix products, arithmetic and copies ran while one was open for 4% of the time, Pallas kernels for 26%

profile of v1, /device:TPU:0, one launch (start us, length us, event | category | flops | bytes accessed | tf_op | source)
XLA Modules:
  0.0 62.4 jit_solution(9845728606697042589)
XLA Ops:
  0.7 3.0 %collective-permute-start.7 = (bf16[64,5120]{1,0:T(8,128)(2,1)}, bf16[64,5120]{1,0:T(8,128)(2,1)S(1)}, u32[]{:S(2)}, u32[]{:S(2)}) collective-permute-start(bf16[64,5120]{1,0:T(8,128)(2,1)} %bitcast.22), channel_id=1, source_target_pairs={{0,1},{1,0},{2,3},{3,2},{4,6},{5,7},{6,4},{7,5},{8,9},{9,8},{10,11... | collective-permute-start | bytes 1966088 | tf_op jit(solution)/shard_map/ppermute | solution.py:267
  3.7 0.9 %pad_maximum_fusion.2.refs_5_ = bf16[2,256,128]{2,1,0:T(8,128)(2,1)S(1)} fusion(bf16[1,256,128]{2,1,0:T(8,128)(2,1)} %bitcast.28, bf16[1,256,128]{2,1,0:T(8,128)(2,1)} %bitcast.29), kind=kLoop, calls=%fused_computation.5 | loop fusion | flops 65536 | bytes 262144 | tf_op jit(solution)/shard_map/stack | solution.py:287
  4.6 2.7 %collective-permute-start.4 = (bf16[2,256,128]{2,1,0:T(8,128)(2,1)S(1)}, bf16[2,256,128]{2,1,0:T(8,128)(2,1)S(1)}, u32[]{:S(2)}, u32[]{:S(2)}) collective-permute-start(bf16[2,256,128]{2,1,0:T(8,128)(2,1)S(1)} %pad_maximum_fusion.2.refs_5_), channel_id=1, source_target_pairs={{0,16},{4,20},{8,24},{12,28},{16,0},{20,4},{24,8},{28,12},{1,17},{... | collective-permute-start | bytes 393224 | tf_op jit(solution)/shard_map/ppermute | solution.py:19
  7.2 1.3 %collective-permute-start.3 = (bf16[2,256,128]{2,1,0:T(8,128)(2,1)S(1)}, bf16[2,256,128]{2,1,0:T(8,128)(2,1)S(1)}, u32[]{:S(2)}, u32[]{:S(2)}) collective-permute-start(bf16[2,256,128]{2,1,0:T(8,128)(2,1)S(1)} %pad_maximum_fusion.2.refs_5_), channel_id=1, source_target_pairs={{0,24},{4,28},{8,16},{12,20},{16,8},{20,12},{24,0},{28,4},{1,25},{... | collective-permute-start | bytes 393224 | tf_op jit(solution)/shard_map/ppermute | solution.py:19
  8.6 0.2 collective-permute-start.1
  9.5 7.8 %collective-permute-done.4.refs_10_.refs_6_ = bf16[2,256,128]{2,1,0:T(8,128)(2,1)S(1)} collective-permute-done((bf16[2,256,128]{2,1,0:T(8,128)(2,1)S(1)}, bf16[2,256,128]{2,1,0:T(8,128)(2,1)S(1)}, u32[]{:S(2)}, u32[]{:S(2)}) %collective-permute-start.4) | collective-permute-done | bytes 131104 | tf_op jit(solution)/shard_map/ppermute | solution.py:19
  17.3 0.5 collective-permute-start.8
  17.8 1.6 %collective-permute-start.9 = (bf16[64,5120]{1,0:T(8,128)(2,1)S(1)}, bf16[64,5120]{1,0:T(8,128)(2,1)S(1)}, u32[]{:S(2)}, u32[]{:S(2)}) collective-permute-start(bf16[64,5120]{1,0:T(8,128)(2,1)S(1)} %collective-permute-done.7.refs_1_), channel_id=1, source_target_pairs={{0,2},{1,3},{2,0},{3,1},{4,5},{5,4},{6,7},{7,6},{8,10},{9,11},{10,... | collective-permute-start | bytes 1966088 | tf_op jit(solution)/shard_map/ppermute | solution.py:267
  19.3 0.5 fusion
  20.0 0.5 collective-permute-start.5
  20.5 0.1 collective-permute-start.2
  20.6 0.1 pad_maximum_fusion
  20.7 0.6 collective-permute-done.6.refs_12_.refs_6_
  21.3 0.2 collective-permute-done.5.refs_11_.refs_5_
  21.5 0.3 collective-permute-done.2.refs_8_.refs_5_
  21.8 0.8 %copy-done.4 = bf16[1,256,1,128]{3,1,2,0:T(8,128)(2,1)S(1)} copy-done((bf16[1,256,1,128]{3,1,2,0:T(8,128)(2,1)S(1)}, bf16[1,256,1,128]{3,1,2,0:T(8,128)(2,1)}, u32[]{:S(2)}) %copy-start.4) | copy-done | bytes 65560
  22.7 7.4 %shard_map.137 = (bf16[2,256,1280]{2,1,0:T(8,128)(2,1)S(1)}, bf16[2,256,1280]{2,1,0:T(8,128)(2,1)S(1)}, bf16[2,256,1280]{2,1,0:T(8,128)(2,1)S(1)}, bf16[1,256,12...) custom-call(bf16[5,256,128]{2,1,0:T(8,128)(2,1)S(1)} %bitcast.25, ...), custom_call_target="tpu_custom_call" | custom-call | flops 1509949440 | bytes 2949120 | tf_op jit(solution)/shard_map/pallas_call | solution.py:300
  30.1 5.0 %collective-permute-done.9.refs_3_ = bf16[64,5120]{1,0:T(8,128)(2,1)S(1)} collective-permute-done((bf16[64,5120]{1,0:T(8,128)(2,1)S(1)}, bf16[64,5120]{1,0:T(8,128)(2,1)S(1)}, u32[]{:S(2)}, u32[]{:S(2)}) %collective-permute-start.9) | collective-permute-done | bytes 655392 | tf_op jit(solution)/shard_map/ppermute | solution.py:267
  35.1 1.1 %copy-done.1 = bf16[1,64,5120]{2,1,0:T(8,128)(2,1)S(1)} copy-done((bf16[1,64,5120]{2,1,0:T(8,128)(2,1)S(1)}, bf16[1,64,5120]{2,1,0:T(8,128)(2,1)}, u32[]{:S(2)}) %copy-start.1) | copy-done | bytes 655384
  36.2 5.1 %shard_map.138 = (bf16[5,256,128]{2,1,0:T(8,128)(2,1)S(1)}, bf16[128,1280]{1,0:T(8,128)(2,1)S(1)}, f32[1,1280]{1,0:T(1,128)S(1)}) custom-call(s32[4]{0:T(128)S(1)} %fusion.1.slots_ref, bf16[64,5120]{1,0:T(8,128)(2,1)S(1)} %bitcast.24, bf16[64,5120]{1,0:T(8,128)(2,1)S(1)} %collective-permute-done.7.refs_1_, ...), custom_call_target="tpu_custom_call" | custom-call | flops 1677721600 | bytes 3276800 | tf_op jit(solution)/shard_map/pallas_call | solution.py:149
  41.4 2.1 %shard_map.140 = (bf16[2,2,256,128]{3,2,1,0:T(8,128)(2,1)S(1)}, f32[128,1280]{1,0:T(8,128)S(1)}) custom-call(bf16[2,256,1280]{2,1,0:T(8,128)(2,1)S(1)} %get-tuple-element.37.refs_0_, bf16[5,256,128]{2,1,0:T(8,128)(2,1)S(1)} %get-tuple-element.29.refs_1_, bf16[5,256,128]{2,1,0:T(8,128)(2,1)S(1)} %get-tuple-element.31.refs_2_, ...), custom_call_target="tpu_custom_call" | custom-call | flops 671088640 | bytes 1310720 | tf_op jit(solution)/shard_map/pallas_call | solution.py:240
  43.6 2.2 %shard_map.139 = (bf16[2,2,256,128]{3,2,1,0:T(8,128)(2,1)S(1)}, f32[128,1280]{1,0:T(8,128)S(1)}) custom-call(bf16[2,256,1280]{2,1,0:T(8,128)(2,1)S(1)} %get-tuple-element.34.refs_0_, bf16[5,256,128]{2,1,0:T(8,128)(2,1)S(1)} %get-tuple-element.29.refs_1_, bf16[5,256,128]{2,1,0:T(8,128)(2,1)S(1)} %get-tuple-element.31.refs_2_, ...), custom_call_target="tpu_custom_call" | custom-call | flops 671088640 | bytes 1310720 | tf_op jit(solution)/shard_map/pallas_call | solution.py:240
  45.7 0.6 collective-permute-start.10
  46.3 2.3 %shard_map.141 = (bf16[2,256,128]{2,1,0:T(8,128)(2,1)S(1)}, bf16[2,256,128]{2,1,0:T(8,128)(2,1)S(1)}, f32[128,1280]{1,0:T(8,128)S(1)}) custom-call(bf16[2,256,1280]{2,1,0:T(8,128)(2,1)S(1)} %get-tuple-element.39.refs_0_, bf16[5,256,128]{2,1,0:T(8,128)(2,1)S(1)} %get-tuple-element.29.refs_1_, bf16[5,256,128]{2,1,0:T(8,128)(2,1)S(1)} %get-tuple-element.31.refs_2_, ...), custom_call_target="tpu_custom_call" | custom-call | flops 671088640 | bytes 1310720 | tf_op jit(solution)/shard_map/pallas_call | solution.py:240
  48.6 2.5 %collective-permute-start.12 = (bf16[2,256,128]{2,1,0:T(8,128)(2,1)S(1)}, bf16[2,256,128]{2,1,0:T(8,128)(2,1)S(1)}, u32[]{:S(2)}, u32[]{:S(2)}) collective-permute-start(bf16[2,256,128]{2,1,0:T(8,128)(2,1)S(1)} %get-tuple-element.48), channel_id=1, source_target_pairs={{0,24},{4,28},{8,16},{12,20},{16,8},{20,12},{24,0},{28,4},{1,25},{... | collective-permute-start | bytes 393224 | tf_op jit(solution)/shard_map/ppermute | solution.py:19
  51.2 1.2 %shard_map.142 = (bf16[2,256,128]{2,1,0:T(8,128)(2,1)S(1)}, f32[128,1280]{1,0:T(8,128)S(1)}) custom-call(bf16[1,256,1280]{2,1,0:T(8,128)(2,1)S(1)} %get-tuple-element.43.refs_0_, bf16[5,256,128]{2,1,0:T(8,128)(2,1)S(1)} %get-tuple-element.29.refs_1_, bf16[5,256,128]{2,1,0:T(8,128)(2,1)S(1)} %get-tuple-element.31.refs_2_, ...), custom_call_target="tpu_custom_call" | custom-call | flops 335544320 | bytes 655360 | tf_op jit(solution)/shard_map/pallas_call | solution.py:240
  52.4 2.0 %collective-permute-start.14 = (bf16[2,256,128]{2,1,0:T(8,128)(2,1)S(1)}, bf16[2,256,128]{2,1,0:T(8,128)(2,1)S(1)}, u32[]{:S(2)}, u32[]{:S(2)}) collective-permute-start(bf16[2,256,128]{2,1,0:T(8,128)(2,1)S(1)} %get-tuple-element.50), channel_id=1, source_target_pairs={{0,8},{4,12},{8,0},{12,4},{16,24},{20,28},{24,16},{28,20},{1,9},{5... | collective-permute-start | bytes 393224 | tf_op jit(solution)/shard_map/ppermute | solution.py:19
  54.4 3.0 %shard_map.143 = (f32[2,256,128]{2,1,0:T(8,128)S(1)}, bf16[2,256,128]{2,1,0:T(8,128)(2,1)S(1)}, bf16[5,256,128]{2,1,0:T(8,128)(2,1)}) custom-call(bf16[2,256,1280]{2,1,0:T(8,128)(2,1)S(1)} %get-tuple-element.28.refs_0_, bf16[5,256,128]{2,1,0:T(8,128)(2,1)S(1)} %get-tuple-element.29.refs_1_, bf16[5,256,128]{2,1,0:T(8,128)(2,1)S(1)} %get-tuple-element.31.refs_2_, ...), custom_call_target="tpu_custom_call" | custom-call | flops 671088640 | bytes 1310720 | tf_op jit(solution)/shard_map/pallas_call | solution.py:240
  57.5 0.7 %slice_bitcast_fusion.2 = (bf16[1,256,1,128]{3,1,2,0:T(8,128)(2,1)}, bf16[1,256,1,128]{3,1,2,0:T(8,128)(2,1)}) fusion(bf16[2,256,128]{2,1,0:T(8,128)(2,1)S(1)} %get-tuple-element.46), kind=kLoop, calls=%fused_computation.8 | loop fusion | bytes 262144 | tf_op jit(solution)/shard_map/broadcast_in_dim;squeeze | solution.py:342
  58.1 3.5 %collective-permute-done.13 = bf16[2,256,128]{2,1,0:T(8,128)(2,1)S(1)} collective-permute-done((bf16[2,256,128]{2,1,0:T(8,128)(2,1)S(1)}, bf16[2,256,128]{2,1,0:T(8,128)(2,1)S(1)}, u32[]{:S(2)}, u32[]{:S(2)}) %collective-permute-start.13) | collective-permute-done | bytes 131104 | tf_op jit(solution)/shard_map/ppermute | solution.py:19
  61.6 0.1 add_convert_fusion
  61.7 0.7 %slice_bitcast_fusion = (bf16[256,1,128]{2,0,1:T(8,128)(2,1)}, bf16[256,1,128]{2,0,1:T(8,128)(2,1)}) fusion(bf16[2,256,128]{2,1,0:T(8,128)(2,1)S(1)} %add_convert_fusion), kind=kLoop, calls=%fused_computation.6 | loop fusion | bytes 262144 | tf_op jit(solution)/shard_map/broadcast_in_dim;squeeze | solution.py:344
  (24 shorter events, 0.2 us)
Async XLA Ops:
  0.6 21.2 %copy-start.3 = (bf16[1,256,1,128]{3,1,2,0:T(8,128)(2,1)S(1)}, bf16[1,256,1,128]{3,1,2,0:T(8,128)(2,1)}, u32[]{:S(2)}) copy-start(bf16[1,256,1,128]{3,1,2,0:T(8,128)(2,1)} %param.13) | copy-start | bytes 196612
  0.6 21.2 %copy-start.2 = (bf16[1,256,1,5,128]{4,1,3,2,0:T(8,128)(2,1)S(1)}, bf16[1,256,1,5,128]{4,1,3,2,0:T(8,128)(2,1)}, u32[]{:S(2)}) copy-start(bf16[1,256,1,5,128]{4,1,3,2,0:T(8,128)(2,1)} %param.12) | copy-start | bytes 983044
  0.7 17.1 %collective-permute-start.7 = (bf16[64,5120]{1,0:T(8,128)(2,1)}, bf16[64,5120]{1,0:T(8,128)(2,1)S(1)}, u32[]{:S(2)}, u32[]{:S(2)}) collective-permute-start(bf16[64,5120]{1,0:T(8,128)(2,1)} %bitcast.22), channel_id=1, source_target_pairs={{0,1},{1,0},{2,3},{3,2},{4,6},{5,7},{6,4},{7,5},{8,9},{9,8},{10,11... | collective-permute-start | bytes 1966088 | tf_op jit(solution)/shard_map/ppermute | solution.py:267
  4.6 12.7 %collective-permute-start.4 = (bf16[2,256,128]{2,1,0:T(8,128)(2,1)S(1)}, bf16[2,256,128]{2,1,0:T(8,128)(2,1)S(1)}, u32[]{:S(2)}, u32[]{:S(2)}) collective-permute-start(bf16[2,256,128]{2,1,0:T(8,128)(2,1)S(1)} %pad_maximum_fusion.2.refs_5_), channel_id=1, source_target_pairs={{0,16},{4,20},{8,24},{12,28},{16,0},{20,4},{24,8},{28,12},{1,17},{... | collective-permute-start | bytes 393224 | tf_op jit(solution)/shard_map/ppermute | solution.py:19
  7.2 12.6 %collective-permute-start.3 = (bf16[2,256,128]{2,1,0:T(8,128)(2,1)S(1)}, bf16[2,256,128]{2,1,0:T(8,128)(2,1)S(1)}, u32[]{:S(2)}, u32[]{:S(2)}) collective-permute-start(bf16[2,256,128]{2,1,0:T(8,128)(2,1)S(1)} %pad_maximum_fusion.2.refs_5_), channel_id=1, source_target_pairs={{0,24},{4,28},{8,16},{12,20},{16,8},{20,12},{24,0},{28,4},{1,25},{... | collective-permute-start | bytes 393224 | tf_op jit(solution)/shard_map/ppermute | solution.py:19
  8.6 11.4 %collective-permute-start.1 = (bf16[2,256,128]{2,1,0:T(8,128)(2,1)S(1)}, bf16[2,256,128]{2,1,0:T(8,128)(2,1)S(1)}, u32[]{:S(2)}, u32[]{:S(2)}) collective-permute-start(bf16[2,256,128]{2,1,0:T(8,128)(2,1)S(1)} %pad_maximum_fusion.2.refs_5_), channel_id=1, source_target_pairs={{0,8},{4,12},{8,0},{12,4},{16,24},{20,28},{24,16},{28,20},{1,9},{5... | collective-permute-start | bytes 393224 | tf_op jit(solution)/shard_map/ppermute | solution.py:19
  8.8 11.7 %collective-permute-start = (bf16[2,256,128]{2,1,0:T(8,128)(2,1)S(1)}, bf16[2,256,128]{2,1,0:T(8,128)(2,1)S(1)}, u32[]{:S(2)}, u32[]{:S(2)}) collective-permute-start(bf16[2,256,128]{2,1,0:T(8,128)(2,1)S(1)} %pad_maximum_fusion.2.refs_5_), channel_id=1, source_target_pairs={{0,4},{4,0},{8,12},{12,8},{16,20},{20,16},{24,28},{28,24},{1,5},{5... | collective-permute-start | bytes 393224 | tf_op jit(solution)/shard_map/ppermute | solution.py:19
  17.3 12.8 %collective-permute-start.8 = (bf16[64,5120]{1,0:T(8,128)(2,1)}, bf16[64,5120]{1,0:T(8,128)(2,1)S(1)}, u32[]{:S(2)}, u32[]{:S(2)}) collective-permute-start(bf16[64,5120]{1,0:T(8,128)(2,1)} %bitcast.23), channel_id=1, source_target_pairs={{0,2},{1,3},{2,0},{3,1},{4,5},{5,4},{6,7},{7,6},{8,10},{9,11},{10,... | collective-permute-start | bytes 1966088 | tf_op jit(solution)/shard_map/ppermute | solution.py:267
  17.8 17.4 %collective-permute-start.9 = (bf16[64,5120]{1,0:T(8,128)(2,1)S(1)}, bf16[64,5120]{1,0:T(8,128)(2,1)S(1)}, u32[]{:S(2)}, u32[]{:S(2)}) collective-permute-start(bf16[64,5120]{1,0:T(8,128)(2,1)S(1)} %collective-permute-done.7.refs_1_), channel_id=1, source_target_pairs={{0,2},{1,3},{2,0},{3,1},{4,5},{5,4},{6,7},{7,6},{8,10},{9,11},{10,... | collective-permute-start | bytes 1966088 | tf_op jit(solution)/shard_map/ppermute | solution.py:267
  19.3 15.8 %copy-start = (bf16[1,5,128,5120]{3,2,1,0:T(8,128)(2,1)S(1)}, bf16[1,5,128,5120]{3,2,1,0:T(8,128)(2,1)}, u32[]{:S(2)}) copy-start(bf16[1,5,128,5120]{3,2,1,0:T(8,128)(2,1)} %param.11) | copy-start | bytes 19660804
  19.9 1.4 %collective-permute-start.6 = (bf16[2,256,128]{2,1,0:T(8,128)(2,1)S(1)}, bf16[2,256,128]{2,1,0:T(8,128)(2,1)S(1)}, u32[]{:S(2)}, u32[]{:S(2)}) collective-permute-start(bf16[2,256,128]{2,1,0:T(8,128)(2,1)S(1)} %collective-permute-done.4.refs_10_.refs_6_), channel_id=1, source_target_pairs={{0,4},{4,0},{8,12},{12,8},{16,20},{20,16},{24,28},{28,24},{1,5},{5... | collective-permute-start | bytes 393224 | tf_op jit(solution)/shard_map/ppermute | solution.py:19
  20.0 1.5 %collective-permute-start.5 = (bf16[2,256,128]{2,1,0:T(8,128)(2,1)S(1)}, bf16[2,256,128]{2,1,0:T(8,128)(2,1)S(1)}, u32[]{:S(2)}, u32[]{:S(2)}) collective-permute-start(bf16[2,256,128]{2,1,0:T(8,128)(2,1)S(1)} %collective-permute-done.3.refs_9_.refs_5_), channel_id=1, source_target_pairs={{0,4},{4,0},{8,12},{12,8},{16,20},{20,16},{24,28},{28,24},{1,5},{5... | collective-permute-start | bytes 393224 | tf_op jit(solution)/shard_map/ppermute | solution.py:19
  20.5 1.3 %collective-permute-start.2 = (bf16[2,256,128]{2,1,0:T(8,128)(2,1)S(1)}, bf16[2,256,128]{2,1,0:T(8,128)(2,1)S(1)}, u32[]{:S(2)}, u32[]{:S(2)}) collective-permute-start(bf16[2,256,128]{2,1,0:T(8,128)(2,1)S(1)} %collective-permute-done.1.refs_7_.refs_5_), channel_id=1, source_target_pairs={{0,4},{4,0},{8,12},{12,8},{16,20},{20,16},{24,28},{28,24},{1,5},{5... | collective-permute-start | bytes 393224 | tf_op jit(solution)/shard_map/ppermute | solution.py:19
  21.8 0.8 %copy-start.4 = (bf16[1,256,1,128]{3,1,2,0:T(8,128)(2,1)S(1)}, bf16[1,256,1,128]{3,1,2,0:T(8,128)(2,1)}, u32[]{:S(2)}) copy-start(bf16[1,256,1,128]{3,1,2,0:T(8,128)(2,1)} %param.14) | copy-start | bytes 196612
  35.1 1.1 %copy-start.1 = (bf16[1,64,5120]{2,1,0:T(8,128)(2,1)S(1)}, bf16[1,64,5120]{2,1,0:T(8,128)(2,1)}, u32[]{:S(2)}) copy-start(bf16[1,64,5120]{2,1,0:T(8,128)(2,1)} %param.10) | copy-start | bytes 1966084
  43.5 2.8 %collective-permute-start.11 = (bf16[2,2,256,128]{3,2,1,0:T(8,128)(2,1)S(1)}, bf16[2,2,256,128]{3,2,1,0:T(8,128)(2,1)S(1)}, u32[]{:S(2)}, u32[]{:S(2)}) collective-permute-start(bf16[2,2,256,128]{3,2,1,0:T(8,128)(2,1)S(1)} %get-tuple-element.40), channel_id=1, source_target_pairs={{0,4},{4,0},{8,12},{12,8},{16,20},{20,16},{24,28},{28,24},{1,5},{5... | collective-permute-start | bytes 786440 | tf_op jit(solution)/shard_map/ppermute | solution.py:19
  45.7 5.4 %collective-permute-start.10 = (bf16[2,2,256,128]{3,2,1,0:T(8,128)(2,1)S(1)}, bf16[2,2,256,128]{3,2,1,0:T(8,128)(2,1)S(1)}, u32[]{:S(2)}, u32[]{:S(2)}) collective-permute-start(bf16[2,2,256,128]{3,2,1,0:T(8,128)(2,1)S(1)} %get-tuple-element.35), channel_id=1, source_target_pairs={{0,4},{4,0},{8,12},{12,8},{16,20},{20,16},{24,28},{28,24},{1,5},{5... | collective-permute-start | bytes 786440 | tf_op jit(solution)/shard_map/ppermute | solution.py:19
  48.6 9.5 %collective-permute-start.12 = (bf16[2,256,128]{2,1,0:T(8,128)(2,1)S(1)}, bf16[2,256,128]{2,1,0:T(8,128)(2,1)S(1)}, u32[]{:S(2)}, u32[]{:S(2)}) collective-permute-start(bf16[2,256,128]{2,1,0:T(8,128)(2,1)S(1)} %get-tuple-element.48), channel_id=1, source_target_pairs={{0,24},{4,28},{8,16},{12,20},{16,8},{20,12},{24,0},{28,4},{1,25},{... | collective-permute-start | bytes 393224 | tf_op jit(solution)/shard_map/ppermute | solution.py:19
  51.2 10.5 %collective-permute-start.13 = (bf16[2,256,128]{2,1,0:T(8,128)(2,1)S(1)}, bf16[2,256,128]{2,1,0:T(8,128)(2,1)S(1)}, u32[]{:S(2)}, u32[]{:S(2)}) collective-permute-start(bf16[2,256,128]{2,1,0:T(8,128)(2,1)S(1)} %get-tuple-element.49), channel_id=1, source_target_pairs={{0,16},{4,20},{8,24},{12,28},{16,0},{20,4},{24,8},{28,12},{1,17},{... | collective-permute-start | bytes 393224 | tf_op jit(solution)/shard_map/ppermute | solution.py:19
  52.4 9.2 %collective-permute-start.14 = (bf16[2,256,128]{2,1,0:T(8,128)(2,1)S(1)}, bf16[2,256,128]{2,1,0:T(8,128)(2,1)S(1)}, u32[]{:S(2)}, u32[]{:S(2)}) collective-permute-start(bf16[2,256,128]{2,1,0:T(8,128)(2,1)S(1)} %get-tuple-element.50), channel_id=1, source_target_pairs={{0,8},{4,12},{8,0},{12,4},{16,24},{20,28},{24,16},{28,20},{1,9},{5... | collective-permute-start | bytes 393224 | tf_op jit(solution)/shard_map/ppermute | solution.py:19
